TPU v7x, 256 devices: a whole 4x4x8 slice. The times are simulated.
256 devices in a mesh: member: 16 (over y, x_hi, core), dp: 16 (over z, x_lo).
Axes of the slice: x: 4 (x_hi: 2, x_lo: 2; x = x_hi * 2 + x_lo), y: 4, z: 8, core: 2. Of those that a mesh axis runs over, the one named last changes fastest.
Arguments:
- teacher_tokens: bfloat16 [2752, 1536], P('dp'), may hold values from -100 to 100
- teacher_qkv: bfloat16 [16, 1536, 4608], P('member', None, 'dp'), may hold values from -0.15625 to 0.15625
- student_tokens: bfloat16 [2752, 1024], P('dp'), may hold values from -6 to 6
- student_gain: float32 [1024], replicated, may hold values from 0.1 to 1.9
- w_up: bfloat16 [1024, 4096], P(None, 'member'), may hold values from -0.1875 to 0.1875
- w_down: bfloat16 [1024, 4096], P(None, 'member'), may hold values from -0.09375 to 0.09375
- w_head: bfloat16 [1024, 1536], P(None, 'member'), may hold values from -0.1875 to 0.1875
Outputs:
- grad_up: float32 [1024, 4096], P('dp', 'member')
- grad_down: float32 [1024, 4096], P('dp', 'member')
- grad_head: float32 [1024, 1536], P('dp', 'member')
All inputs are finite; a program needn't handle non-finite values.
Results may differ from a plain program's by a relative error of at most 0.0055.
Values may be sent and summed in bfloat16 or wider, within the bound.
No kernel may reach another device: no remote copies, remote signals or barrier semaphores. Data moves between devices by JAX's collectives and lax.ppermute only.
A program may use at most 192 MiB of HBM per device.

v0:
```python
from functools import partial
import math
import jax
import jax.numpy as jnp
from jax import lax
from jax.sharding import PartitionSpec as P

VALID = 1370
IMAGES = 2


def body(teacher_tokens, teacher_qkv, student_tokens, student_gain, w_up, w_down, w_head):
    tok_rows = teacher_tokens.shape[0]
    feat_width = teacher_tokens.shape[1]
    head_count = feat_width // 64
    own_columns = teacher_qkv[0]
    query_slots = lax.axis_index("dp") * tok_rows + jnp.arange(tok_rows, dtype=jnp.int32)
    query_image = query_slots % IMAGES
    real_query = query_slots // IMAGES < VALID
    projected = jnp.dot(
        teacher_tokens,
        lax.all_gather(own_columns, "dp", axis=1, tiled=True),
        preferred_element_type=jnp.float32,
    ).astype(jnp.bfloat16)
    queries = projected[:, :feat_width].reshape(tok_rows, head_count, 64)
    keys_local = projected[:, feat_width : 2 * feat_width]
    values_local = projected[:, 2 * feat_width :]
    row_max = jnp.full((head_count, tok_rows), -1e30, jnp.float32)
    weighted = jnp.zeros((tok_rows, head_count, 64), jnp.float32)
    key_heads = lax.all_gather(keys_local, "dp", axis=0, tiled=True).reshape(-1, head_count, 64)
    value_heads = lax.all_gather(values_local, "dp", axis=0, tiled=True).reshape(-1, head_count, 64)
    key_slots = jnp.arange(key_heads.shape[0], dtype=jnp.int32)
    allowed = (query_image[:, None] == (key_slots % IMAGES)[None, :]) & (
        key_slots // IMAGES < VALID
    )[None, :]
    scores = (
        jnp.einsum("qhd,khd->hqk", queries, key_heads, preferred_element_type=jnp.float32) * 0.125
    )
    scores = jnp.where(allowed[None], scores, -1e30)
    new_max = jnp.maximum(row_max, jnp.max(scores, axis=-1))
    factor = jnp.exp(row_max - new_max)
    expsc = jnp.where(allowed[None], jnp.exp(scores - new_max[:, :, None]), 0.0)
    denom_sum = jnp.sum(expsc, axis=-1)
    update = jnp.einsum(
        "hqk,khd->qhd", expsc.astype(jnp.bfloat16), value_heads, preferred_element_type=jnp.float32
    )
    weighted = weighted * factor.T[:, :, None] + update
    row_max, denom_sum, weighted = (new_max, denom_sum, weighted)
    context = (weighted / denom_sum.T[:, :, None]).reshape(tok_rows, feat_width)
    member_slot = lax.axis_index("member")
    share_width = feat_width // lax.axis_size("member")
    summed = lax.psum(context, "member")
    row_mean = jnp.mean(summed, axis=-1, keepdims=True)
    mean_square = jnp.mean(summed * summed, axis=-1, keepdims=True)
    full_target = (summed - row_mean) * lax.rsqrt(mean_square - row_mean * row_mean + 1e-06)
    target = lax.dynamic_slice_in_dim(full_target, member_slot * share_width, share_width, 1)
    inputs = student_tokens.astype(jnp.float32)
    in_mean = jnp.mean(inputs, axis=-1, keepdims=True)
    in_var = jnp.mean((inputs - in_mean) ** 2, axis=-1, keepdims=True)
    normed = ((inputs - in_mean) * lax.rsqrt(in_var + 1e-06) * student_gain).astype(jnp.bfloat16)
    pre = jnp.dot(normed, w_up, preferred_element_type=jnp.float32)
    gelu_tanh = partial(jax.nn.gelu, approximate=True)
    hidden = gelu_tanh(pre).astype(jnp.bfloat16)
    branch_part = lax.dot_general(
        hidden, w_down, (((1,), (1,)), ((), ())), preferred_element_type=jnp.float32
    )
    student_out = (inputs + lax.psum(branch_part, "member")).astype(jnp.bfloat16)
    pred = jnp.dot(student_out, w_head, preferred_element_type=jnp.float32)
    pred_grad = jnp.where(
        real_query[:, None], (pred - target) / math.sqrt(IMAGES * VALID), 0.0
    ).astype(jnp.bfloat16)
    grad_head = lax.dot_general(
        student_out, pred_grad, (((0,), (0,)), ((), ())), preferred_element_type=jnp.float32
    )
    out_part = lax.dot_general(
        pred_grad, w_head, (((1,), (1,)), ((), ())), preferred_element_type=jnp.float32
    )
    out_grad = lax.psum(out_part, "member").astype(jnp.bfloat16)
    grad_down = lax.dot_general(
        out_grad, hidden, (((0,), (0,)), ((), ())), preferred_element_type=jnp.float32
    )
    hidden_grad = jnp.dot(out_grad, w_down, preferred_element_type=jnp.float32)
    _, pullback = jax.vjp(gelu_tanh, pre)
    pre_grad = pullback(hidden_grad)[0].astype(jnp.bfloat16)
    grad_up = lax.dot_general(
        normed, pre_grad, (((0,), (0,)), ((), ())), preferred_element_type=jnp.float32
    )
    grad_up, grad_down, grad_head = (
        lax.psum_scatter(grad_up, "dp", scatter_dimension=0, tiled=True),
        lax.psum_scatter(grad_down, "dp", scatter_dimension=0, tiled=True),
        lax.psum_scatter(grad_head, "dp", scatter_dimension=0, tiled=True),
    )
    return (grad_up, grad_down, grad_head)


def solution(mesh):
    in_specs = (
        P("dp", None),
        P("member", None, "dp"),
        P("dp", None),
        P(),
        P(None, "member"),
        P(None, "member"),
        P(None, "member"),
    )
    out_specs = (P("dp", "member"), P("dp", "member"), P("dp", "member"))
    return jax.shard_map(body, mesh=mesh, in_specs=in_specs, out_specs=out_specs, check_vma=False)
```

profile of v0, /device:TPU:8, one launch (start us, length us, event | category | flops | bytes accessed | tf_op | source)
XLA Modules:
  0.0 1197.4 jit_solution(361960012682249767)
XLA Ops:
  7.3 0.7 all-gather.7.cloned.1.call-update
  8.0 303.0 %all-gather.7.cloned.1.call-done = bf16[1,1536,4608]{1,2,0:T(8,128)(2,1)} async-done(((bf16[1,1536,288]{1,2,0:T(8,128)(2,1)}), bf16[1,1536,4608]{1,2,0:T(8,128)(2,1)}) %all-gather.7.cloned.1.call-update) | async-done | bytes 14155792 | tf_op jit(solution)/shard_map/all_gather | solution.py:22
  311.0 9.7 fusion.8
  320.7 1.2 slice_bitcast_fusion.1
  322.0 0.7 all-gather.9.cloned.1.call-update
  322.8 0.1 convert_reduce_fusion
  322.9 0.2 fusion.19
  323.2 0.3 fusion.71
  323.5 1.2 fusion.69
  324.7 0.4 compare_and_fusion
  325.1 0.3 copy.18
  325.4 186.0 %all-gather.11.cloned.1.call-done = bf16[16,172,1536]{2,1,0:T(8,128)(2,1)} async-done(((bf16[1,172,1536]{2,1,0:T(8,128)(2,1)}), bf16[16,172,1536]{2,1,0:T(8,128)(2,1)}) %all-gather.11.cloned.1.call-update) | async-done | bytes 8454160 | tf_op jit(solution)/shard_map/all_gather | solution.py:31
  511.4 17.4 %copy.20 = bf16[16,172,1536]{1,0,2:T(8,128)(2,1)} copy(bf16[16,172,1536]{2,1,0:T(8,128)(2,1)} %all-gather.11.cloned.1.call-done) | data formatting | bytes 16908288 | tf_op jit(solution)/shard_map/all_gather | solution.py:31
  528.8 22.6 %reshape.154 = bf16[2752,24,64]{0,2,1:T(8,128)(2,1)} reshape(bf16[16,172,1536]{1,0,2:T(8,128)(2,1)} %copy.20) | data formatting | bytes 16908288 | tf_op jit(solution)/shard_map/reshape | solution.py:31
  551.4 150.4 %all-gather.9.cloned.1.call-done = bf16[16,172,1536]{2,1,0:T(8,128)(2,1)} async-done(((bf16[1,172,1536]{2,1,0:T(8,128)(2,1)}), bf16[16,172,1536]{2,1,0:T(8,128)(2,1)}) %all-gather.9.cloned.1.call-update) | async-done | bytes 8454160 | tf_op jit(solution)/shard_map/all_gather | solution.py:30
  701.8 17.4 %copy.19 = bf16[16,172,1536]{1,0,2:T(8,128)(2,1)} copy(bf16[16,172,1536]{2,1,0:T(8,128)(2,1)} %all-gather.9.cloned.1.call-done) | data formatting | bytes 16908288 | tf_op jit(solution)/shard_map/all_gather | solution.py:30
  719.2 22.6 %reshape.153 = bf16[2752,24,64]{0,2,1:T(8,128)(2,1)} reshape(bf16[16,172,1536]{1,0,2:T(8,128)(2,1)} %copy.19) | data formatting | bytes 16908288 | tf_op jit(solution)/shard_map/reshape | solution.py:30
  741.8 21.7 %fusion = (f32[24,172]{1,0:T(8,128)S(1)}, f32[24,172,2752]{2,1,0:T(8,128)}) fusion(pred[172,2752]{1,0:T(8,128)(4,1)S(1)} %compare_and_fusion, bf16[172,24,64]{0,2,1:T(8,128)(2,1)S(1)} %bitcast.35, bf16[2752,24,64]{0,2,1:T(8,128)(2,1)} %reshape.153), kind=kOutput, calls=%fused_computation.2 | convolution fusion | flops 1488189440 | bytes 54913408 | tf_op jit(solution)/shard_map/qhd,khd->hqk/dot_general | solution.py:37
  763.5 22.9 %fusion.1 = f32[24,172]{1,0:T(8,128)S(1)} fusion(f32[24,172,2752]{2,1,0:T(8,128)} %get-tuple-element.15, f32[24,172]{1,0:T(8,128)S(1)} %get-tuple-element.11, pred[172,2752]{1,0:T(8,128)(4,1)S(1)} %compare_and_fusion), kind=kLoop, calls=%fused_computation.3 | loop fusion | flops 56797152 | bytes 45947392 | tf_op jit(solution)/shard_map/reduce_sum | solution.py:43
  786.4 20.8 %fusion.11 = f32[172,24,64]{0,2,1:T(8,128)S(1)} fusion(bf16[2752,24,64]{0,2,1:T(8,128)(2,1)} %reshape.154, f32[24,172,2752]{2,1,0:T(8,128)} %get-tuple-element.15, f32[24,172]{1,0:T(8,128)S(1)} %get-tuple-element.11, pred[172,2752]{1,0:T(8,128)(4,1)S(1)} %compare_and_fusion, f32[172,24]{0,1:T(8,128)S(1)} %bitcast.37, f32[172,24]{0,1:T(8,128)S(1)} %get-tuple-element.10), kind=kOutput, calls=%fused_computation.12 | convolution fusion | flops 1511442432 | bytes 55474816 | tf_op jit(solution)/shard_map/hqk,khd->qhd/dot_general | solution.py:44
  807.3 1.5 copy.21
  808.8 144.0 %all-reduce.4.cloned.1.call-done = (f32[172,1536]{1,0:T(8,128)}, f32[172,1024]{1,0:T(8,128)}) async-done(((f32[172,1536]{1,0:T(8,128)}, f32[172,1024]{1,0:T(8,128)}), (f32[172,1536]{1,0:T(8,128)}, f32[172,1024]{1,0:T(8,128)})) %all-reduce.4.cloned.1.call-update) | async-done | bytes 1761296 | tf_op jit(solution)/shard_map/psum | solution.py:52
  952.9 1.5 fusion.73
  954.3 1.4 fusion.16
  955.8 0.2 fusion.74
  956.0 2.3 fusion.66
  958.3 0.0 reduce-scatter.4.cloned.1.call-start
  958.4 77.2 %all-reduce.5 = bf16[172,1024]{1,0:T(8,128)(2,1)S(1)} all-reduce(f32[172,1024]{1,0:T(8,128)S(1)} %fusion.74), channel_id=1, replica_groups=mesh['member'=16,'dp'=16] {'member'}, use_global_device_ids=true, to_apply=%region_8.9 | all-reduce | flops 176128 | bytes 1056768 | tf_op jit(solution)/shard_map/psum | solution.py:78
  1035.6 2.8 fusion.37
  1038.4 1.4 fusion.30
  1039.8 76.7 %reduce-scatter.4.cloned.1.call-done = f32[64,256]{1,0:T(8,128)} async-done(((f32[1024,256]{1,0:T(8,128)}), f32[64,256]{1,0:T(8,128)}) %reduce-scatter.4.cloned.1.call-update) | async-done | bytes 65552 | tf_op jit(solution)/shard_map/reduce_scatter | solution.py:89
  1116.6 74.0 %reduce-scatter.6.cloned.1.call-done = f32[64,256]{1,0:T(8,128)} async-done(((f32[1024,256]{1,0:T(8,128)}), f32[64,256]{1,0:T(8,128)}) %reduce-scatter.6.cloned.1.call-update) | async-done | bytes 65552 | tf_op jit(solution)/shard_map/reduce_scatter | solution.py:90
  (34 shorter events, 0.5 us)
Async XLA Ops:
  7.2 303.8 %copy-start = (bf16[172,1536]{1,0:T(8,128)(2,1)S(1)}, bf16[172,1536]{1,0:T(8,128)(2,1)}, u32[]{:S(2)}) copy-start(bf16[172,1536]{1,0:T(8,128)(2,1)} %param.7) | copy-start | bytes 1585156
  7.2 315.6 %copy-start.2 = (bf16[172,1024]{1,0:T(8,128)(2,1)S(1)}, bf16[172,1024]{1,0:T(8,128)(2,1)}, u32[]{:S(2)}) copy-start(bf16[172,1024]{1,0:T(8,128)(2,1)} %param.9) | copy-start | bytes 1056772
  7.2 316.0 %copy-start.5 = (bf16[1024,256]{1,0:T(8,128)(2,1)S(1)}, bf16[1024,256]{1,0:T(8,128)(2,1)}, u32[]{:S(2)}) copy-start(bf16[1024,256]{1,0:T(8,128)(2,1)} %param.11) | copy-start | bytes 1572868
  7.2 316.0 %copy-start.6 = (f32[1024]{0:T(1024)S(1)}, f32[1024]{0:T(1024)}, u32[]{:S(2)}) copy-start(f32[1024]{0:T(1024)} %param.10) | copy-start | bytes 12292
  7.2 316.3 %copy-start.4 = (bf16[1024,256]{1,0:T(8,128)(2,1)S(1)}, bf16[1024,256]{1,0:T(8,128)(2,1)}, u32[]{:S(2)}) copy-start(bf16[1024,256]{1,0:T(8,128)(2,1)} %param.12) | copy-start | bytes 1572868
  7.2 303.8 %all-gather.7.cloned.1.call-start = ((), (), s32[]{:S(2)}) async-start(), calls=%async_computation.6 | async-start | bytes 15040512 | tf_op jit(solution)/shard_map/all_gather | solution.py:22
  8.0 503.5 %all-gather.11.cloned.1.call-start = ((), (), s32[]{:S(2)}) async-start(), calls=%async_computation.8 | async-start | bytes 9191424 | tf_op jit(solution)/shard_map/all_gather | solution.py:31
  321.9 379.9 %all-gather.9.cloned.1.call-start = ((), (), s32[]{:S(2)}) async-start(), calls=%async_computation.7 | async-start | bytes 9191424 | tf_op jit(solution)/shard_map/all_gather | solution.py:30
  322.7 630.2 %all-reduce.4.cloned.1.call-start = ((), (), s32[]{:S(2)}) async-start(), calls=%async_computation.9 | async-start | bytes 3604480 | tf_op jit(solution)/shard_map/psum | solution.py:52
  786.4 167.9 %copy-start.3 = (bf16[1024,96]{0,1:T(8,128)(2,1)S(1)}, bf16[1024,96]{0,1:T(8,128)(2,1)}, u32[]{:S(2)}) copy-start(bf16[1024,96]{0,1:T(8,128)(2,1)} %param.13) | copy-start | bytes 589828
  786.4 404.2 %copy-start.1 = (bf16[172,1536]{1,0:T(8,128)(2,1)S(1)}, bf16[172,1536]{1,0:T(8,128)(2,1)}, u32[]{:S(2)}) copy-start(bf16[172,1536]{1,0:T(8,128)(2,1)} %param.7) | copy-start | bytes 1585156
  808.8 231.1 %reduce-scatter.8.cloned.1.call-start = ((), (), s32[]{:S(2)}) async-start(), calls=%async_computation.5 | async-start | bytes 557056 | tf_op jit(solution)/shard_map/reduce_scatter | solution.py:91
  958.3 158.2 %reduce-scatter.4.cloned.1.call-start = ((), (), s32[]{:S(2)}) async-start(), calls=%async_computation.3 | async-start | bytes 1114112 | tf_op jit(solution)/shard_map/reduce_scatter | solution.py:89
  1038.4 152.2 %reduce-scatter.6.cloned.1.call-start = ((), (), s32[]{:S(2)}) async-start(), calls=%async_computation.4 | async-start | bytes 1114112 | tf_op jit(solution)/shard_map/reduce_scatter | solution.py:90
Sparse Core Ops, SparseCore 0:
  9.8 301.1 all-gather.6
  322.0 189.3 all-gather.10
  513.2 188.5 all-gather.8
  808.9 143.9 all-reduce.3
  958.4 79.0 reduce-scatter.7
  1040.5 75.9 reduce-scatter.3
  1119.6 70.9 reduce-scatter.5
where the time goes:
time: 1200 us
  waiting for transfers between devices  936 us (78%)
  local copies, waits for them, and re-layouts  83 us (7%)
  blocking collectives  77.2 us (6%)
  matrix products  61.8 us (5%)
  other arithmetic  25.2 us (2%)
  between operations  14.3 us (1%)
    all_gather x1, waiting for transfers between devices, body(): lax.all_gather(own_columns, 'dp', axis=1, tiled=True)  303 us
    all_gather x1, waiting for transfers between devices, body(): lax.all_gather(values_local, 'dp', axis=0, tiled=True)  186 us
    all_gather x1, waiting for transfers between devices, body(): lax.all_gather(keys_local, 'dp', axis=0, tiled=True)  150 us
    psum x1, waiting for transfers between devices, body(): summed = lax.psum(context, 'member')  144 us
    psum x1, blocking collectives, body(): out_grad = lax.psum(out_part, 'member').astype(jnp.bfloat16)  77.2 us
    reduce_scatter x1, waiting for transfers between devices, body(): lax.psum_scatter(grad_up, 'dp', scatter_dimension=0, tiled=True)  76.7 us
    reduce_scatter x1, waiting for transfers between devices, body(): lax.psum_scatter(grad_down, 'dp', scatter_dimension=0, tiled=True)  74 us
  transfers between devices with their start and end apart: 7, of which 6 were waited for; matrix products, arithmetic and copies ran while one was open for 4% of the time, Pallas kernels for 0%

commit v1 on v0

--- a/solution.py
+++ b/solution.py
@@ -4,6 +4,7 @@
 import jax.numpy as jnp
 from jax import lax
 from jax.sharding import PartitionSpec as P
+from jax.lax import all_gather
 
 VALID = 1370
 IMAGES = 2
@@ -49,7 +50,11 @@
     context = (weighted / denom_sum.T[:, :, None]).reshape(tok_rows, feat_width)
     member_slot = lax.axis_index("member")
     share_width = feat_width // lax.axis_size("member")
-    summed = lax.psum(context, "member")
+
+    def carry_masks(frame_in):
+        return jnp.sum(all_gather(frame_in, axis_name="member"), axis=0)
+
+    summed = carry_masks(context)
     row_mean = jnp.mean(summed, axis=-1, keepdims=True)
     mean_square = jnp.mean(summed * summed, axis=-1, keepdims=True)
     full_target = (summed - row_mean) * lax.rsqrt(mean_square - row_mean * row_mean + 1e-06)

time: 1200 us -> 1310 us (1.092)
  waiting for transfers between devices: 936 us -> 1030 us
    all_gather x0 -> x1, waiting for transfers between devices: none -> 111 us  [carry_masks(): return jnp.sum(all_gather(frame_in, axis_name='member'), axis=0)]
    psum x1, waiting for transfers between devices: 144 us -> 129 us  [body(): lax.psum(branch_part, 'member')]
  transfers between devices with their start and end apart: 7 -> 8, of which waited for: 6 -> 7; matrix products, arithmetic and copies ran while one was open for 4% -> 5% of each run, Pallas kernels for 0% -> 0%
where the time goes in v1:
time: 1310 us
  waiting for transfers between devices  1030 us (79%)
  local copies, waits for them, and re-layouts  84 us (6%)
  blocking collectives  74.6 us (6%)
  matrix products  64.6 us (5%)
  other arithmetic  34.8 us (3%)
  between operations  14.3 us (1%)
    all_gather x1, waiting for transfers between devices, body(): lax.all_gather(own_columns, 'dp', axis=1, tiled=True)  303 us
    all_gather x1, waiting for transfers between devices, body(): lax.all_gather(values_local, 'dp', axis=0, tiled=True)  188 us
    all_gather x1, waiting for transfers between devices, body(): lax.all_gather(keys_local, 'dp', axis=0, tiled=True)  150 us
    psum x1, waiting for transfers between devices, body(): lax.psum(branch_part, 'member')  129 us
    all_gather x1, waiting for transfers between devices, carry_masks(): return jnp.sum(all_gather(frame_in, axis_name='member'), axis=0)  111 us
    reduce_scatter x1, waiting for transfers between devices, body(): lax.psum_scatter(grad_up, 'dp', scatter_dimension=0, tiled=True)  75.9 us
    psum x1, blocking collectives, body(): out_grad = lax.psum(out_part, 'member').astype(jnp.bfloat16)  74.6 us
    reduce_scatter x1, waiting for transfers between devices, body(): lax.psum_scatter(grad_down, 'dp', scatter_dimension=0, tiled=True)  74 us
  transfers between devices with their start and end apart: 8, of which 7 were waited for; matrix products, arithmetic and copies ran while one was open for 5% of the time, Pallas kernels for 0%

profile of v1, /device:TPU:8, one launch (start us, length us, event | category | flops | bytes accessed | tf_op | source)
XLA Modules:
  0.0 1305.7 jit_solution(12027609167667116974)
XLA Ops:
  7.2 0.7 all-gather.10.cloned.1.call-update
  8.0 303.0 %all-gather.10.cloned.1.call-done = bf16[1,1536,4608]{1,2,0:T(8,128)(2,1)} async-done(((bf16[1,1536,288]{1,2,0:T(8,128)(2,1)}), bf16[1,1536,4608]{1,2,0:T(8,128)(2,1)}) %all-gather.10.cloned.1.call-update) | async-done | bytes 14155792 | tf_op jit(solution)/shard_map/all_gather | solution.py:23
  311.0 9.7 fusion.8
  320.7 1.2 slice_bitcast_fusion.1
  321.9 0.7 all-gather.12.cloned.1.call-update
  323.4 188.0 %all-gather.14.cloned.1.call-done = bf16[16,172,1536]{2,1,0:T(8,128)(2,1)} async-done(((bf16[1,172,1536]{2,1,0:T(8,128)(2,1)}), bf16[16,172,1536]{2,1,0:T(8,128)(2,1)}) %all-gather.14.cloned.1.call-update) | async-done | bytes 8454160 | tf_op jit(solution)/shard_map/all_gather | solution.py:32
  511.4 17.4 %copy.18 = bf16[16,172,1536]{1,0,2:T(8,128)(2,1)} copy(bf16[16,172,1536]{2,1,0:T(8,128)(2,1)} %all-gather.14.cloned.1.call-done) | data formatting | bytes 16908288 | tf_op jit(solution)/shard_map/all_gather | solution.py:32
  528.8 22.6 %reshape.151 = bf16[2752,24,64]{0,2,1:T(8,128)(2,1)} reshape(bf16[16,172,1536]{1,0,2:T(8,128)(2,1)} %copy.18) | data formatting | bytes 16908288 | tf_op jit(solution)/shard_map/reshape | solution.py:32
  551.4 150.4 %all-gather.12.cloned.1.call-done = bf16[16,172,1536]{2,1,0:T(8,128)(2,1)} async-done(((bf16[1,172,1536]{2,1,0:T(8,128)(2,1)}), bf16[16,172,1536]{2,1,0:T(8,128)(2,1)}) %all-gather.12.cloned.1.call-update) | async-done | bytes 8454160 | tf_op jit(solution)/shard_map/all_gather | solution.py:31
  701.8 17.4 %copy.17 = bf16[16,172,1536]{1,0,2:T(8,128)(2,1)} copy(bf16[16,172,1536]{2,1,0:T(8,128)(2,1)} %all-gather.12.cloned.1.call-done) | data formatting | bytes 16908288 | tf_op jit(solution)/shard_map/all_gather | solution.py:31
  719.2 22.6 %reshape.150 = bf16[2752,24,64]{0,2,1:T(8,128)(2,1)} reshape(bf16[16,172,1536]{1,0,2:T(8,128)(2,1)} %copy.17) | data formatting | bytes 16908288 | tf_op jit(solution)/shard_map/reshape | solution.py:31
  741.8 21.4 %fusion = (f32[24,172]{1,0:T(8,128)S(1)}, f32[24,172,2752]{2,1,0:T(8,128)}) fusion(pred[172,2752]{1,0:T(8,128)(4,1)S(1)} %compare_and_fusion, bf16[172,24,64]{0,2,1:T(8,128)(2,1)S(1)} %bitcast.35, bf16[2752,24,64]{0,2,1:T(8,128)(2,1)} %reshape.150), kind=kOutput, calls=%fused_computation.2 | convolution fusion | flops 1488189440 | bytes 54913408 | tf_op jit(solution)/shard_map/qhd,khd->hqk/dot_general | solution.py:38
  763.2 22.9 %fusion.1 = f32[24,172]{1,0:T(8,128)S(1)} fusion(f32[24,172,2752]{2,1,0:T(8,128)} %get-tuple-element.13, f32[24,172]{1,0:T(8,128)S(1)} %get-tuple-element.9, pred[172,2752]{1,0:T(8,128)(4,1)S(1)} %compare_and_fusion), kind=kLoop, calls=%fused_computation.3 | loop fusion | flops 56797152 | bytes 45947392 | tf_op jit(solution)/shard_map/reduce_sum | solution.py:44
  786.2 20.8 %fusion.11 = f32[172,24,64]{0,2,1:T(8,128)S(1)} fusion(bf16[2752,24,64]{0,2,1:T(8,128)(2,1)} %reshape.151, f32[24,172,2752]{2,1,0:T(8,128)} %get-tuple-element.13, f32[24,172]{1,0:T(8,128)S(1)} %get-tuple-element.9, pred[172,2752]{1,0:T(8,128)(4,1)S(1)} %compare_and_fusion, f32[172,24]{0,1:T(8,128)S(1)} %bitcast.37, f32[172,24]{0,1:T(8,128)S(1)} %get-tuple-element.8), kind=kOutput, calls=%fused_computation.12 | convolution fusion | flops 1511442432 | bytes 55474816 | tf_op jit(solution)/shard_map/hqk,khd->qhd/dot_general | solution.py:45
  807.0 1.4 copy.19
  809.0 1.4 fusion.71
  810.4 0.7 copy-done.3
  811.0 1.2 fusion.69
  812.3 0.6 fusion.56
  812.9 111.3 %all-gather.8.cloned.1.call-done = f32[16,172,1536]{2,1,0:T(8,128)} async-done(((f32[1,172,1536]{2,1,0:T(8,128)}), f32[16,172,1536]{2,1,0:T(8,128)}) %all-gather.8.cloned.1.call-update) | async-done | bytes 16908304 | tf_op jit(solution)/shard_map/all_gather | solution.py:55
  924.3 9.5 fusion.73
  933.8 0.5 copy.22
  934.5 0.7 broadcast_multiply_fusion
  935.2 128.9 %all-reduce.3.cloned.1.call-done = f32[172,1024]{1,0:T(8,128)} async-done(((f32[172,1024]{1,0:T(8,128)}), f32[172,1024]{1,0:T(8,128)}) %all-reduce.3.cloned.1.call-update) | async-done | bytes 704528 | tf_op jit(solution)/shard_map/psum | solution.py:72
  1064.1 1.5 fusion.16
  1065.6 1.2 fusion.74
  1066.7 2.3 fusion.66
  1069.1 74.6 %all-reduce.4 = bf16[172,1024]{1,0:T(8,128)(2,1)S(1)} all-reduce(f32[172,1024]{1,0:T(8,128)S(1)} %fusion.74), channel_id=1, replica_groups=mesh['member'=16,'dp'=16] {'member'}, use_global_device_ids=true, to_apply=%region_8.9 | all-reduce | flops 176128 | bytes 1056768 | tf_op jit(solution)/shard_map/psum | solution.py:83
  1143.7 2.8 fusion.37
  1146.6 2.3 fusion.30
  1149.0 75.9 %reduce-scatter.4.cloned.1.call-done = f32[64,256]{1,0:T(8,128)} async-done(((f32[1024,256]{1,0:T(8,128)}), f32[64,256]{1,0:T(8,128)}) %reduce-scatter.4.cloned.1.call-update) | async-done | bytes 65552 | tf_op jit(solution)/shard_map/reduce_scatter | solution.py:94
  1224.9 74.0 %reduce-scatter.6.cloned.1.call-done = f32[64,256]{1,0:T(8,128)} async-done(((f32[1024,256]{1,0:T(8,128)}), f32[64,256]{1,0:T(8,128)}) %reduce-scatter.6.cloned.1.call-update) | async-done | bytes 65552 | tf_op jit(solution)/shard_map/reduce_scatter | solution.py:95
  (41 shorter events, 1.8 us)
Async XLA Ops:
  7.2 303.8 %copy-start = (bf16[172,1536]{1,0:T(8,128)(2,1)S(1)}, bf16[172,1536]{1,0:T(8,128)(2,1)}, u32[]{:S(2)}) copy-start(bf16[172,1536]{1,0:T(8,128)(2,1)} %param.7) | copy-start | bytes 1585156
  7.2 303.8 %all-gather.10.cloned.1.call-start = ((), (), s32[]{:S(2)}) async-start(), calls=%async_computation.8 | async-start | bytes 15040512 | tf_op jit(solution)/shard_map/all_gather | solution.py:23
  7.9 503.5 %all-gather.14.cloned.1.call-start = ((), (), s32[]{:S(2)}) async-start(), calls=%async_computation.10 | async-start | bytes 9191424 | tf_op jit(solution)/shard_map/all_gather | solution.py:32
  321.9 379.9 %all-gather.12.cloned.1.call-start = ((), (), s32[]{:S(2)}) async-start(), calls=%async_computation.9 | async-start | bytes 9191424 | tf_op jit(solution)/shard_map/all_gather | solution.py:31
  322.6 601.6 %all-gather.8.cloned.1.call-start = ((), (), s32[]{:S(2)}) async-start(), calls=%async_computation.4 | async-start | bytes 18382848 | tf_op jit(solution)/shard_map/all_gather | solution.py:55
  786.2 22.4 %copy-start.2 = (bf16[172,1024]{1,0:T(8,128)(2,1)S(1)}, bf16[172,1024]{1,0:T(8,128)(2,1)}, u32[]{:S(2)}) copy-start(bf16[172,1024]{1,0:T(8,128)(2,1)} %param.9) | copy-start | bytes 1056772
  786.2 22.8 %copy-start.7 = (f32[1024]{0:T(1024)S(1)}, f32[1024]{0:T(1024)}, u32[]{:S(2)}) copy-start(f32[1024]{0:T(1024)} %param.10) | copy-start | bytes 12292
  786.2 24.9 %copy-start.4 = (bf16[1024,256]{1,0:T(8,128)(2,1)S(1)}, bf16[1024,256]{1,0:T(8,128)(2,1)}, u32[]{:S(2)}) copy-start(bf16[1024,256]{1,0:T(8,128)(2,1)} %param.12) | copy-start | bytes 1572868
  808.5 255.6 %all-reduce.3.cloned.1.call-start = ((), (), s32[]{:S(2)}) async-start(), calls=%async_computation.3 | async-start | bytes 1441792 | tf_op jit(solution)/shard_map/psum | solution.py:72
  808.7 3.5 copy-start.5
  809.0 3.3 copy-start.6
  810.4 0.7 copy-start.3
  812.3 336.7 %reduce-scatter.8.cloned.1.call-start = ((), (), s32[]{:S(2)}) async-start(), calls=%async_computation.7 | async-start | bytes 557056 | tf_op jit(solution)/shard_map/reduce_scatter | solution.py:96
  812.9 485.9 %copy-start.1 = (bf16[172,1536]{1,0:T(8,128)(2,1)S(1)}, bf16[172,1536]{1,0:T(8,128)(2,1)}, u32[]{:S(2)}) copy-start(bf16[172,1536]{1,0:T(8,128)(2,1)} %param.7) | copy-start | bytes 1585156
  1069.0 155.9 %reduce-scatter.4.cloned.1.call-start = ((), (), s32[]{:S(2)}) async-start(), calls=%async_computation.5 | async-start | bytes 1114112 | tf_op jit(solution)/shard_map/reduce_scatter | solution.py:94
  1146.5 152.3 %reduce-scatter.6.cloned.1.call-start = ((), (), s32[]{:S(2)}) async-start(), calls=%async_computation.6 | async-start | bytes 1114112 | tf_op jit(solution)/shard_map/reduce_scatter | solution.py:95
Sparse Core Ops, SparseCore 0:
  9.8 301.1 all-gather.9
  322.0 189.3 all-gather.13
  513.2 188.5 all-gather.11
  808.6 115.5 all-gather.7
  926.7 137.2 all-reduce.2
  1069.1 76.8 reduce-scatter.7
  1149.1 75.7 reduce-scatter.3
  1228.0 70.8 reduce-scatter.5
